TPU v7x, 32 devices: a whole 2x2x4 slice. The times are simulated.
32 devices in a mesh: head: 4 (over z), tok: 8 (over y, x, core).
Axes of the slice: x: 2, y: 2, z: 4, core: 2. Of those that a mesh axis runs over, the one named last changes fastest.
Arguments:
- video_q: bfloat16 [7168, 2048], P('tok', 'head'), may hold values from -6 to 6
- video_k: bfloat16 [7168, 2048], P('tok', 'head'), may hold values from -6 to 6
- video_v: bfloat16 [7168, 2048], P('tok', 'head'), may hold values from -6 to 6
- audio_q: bfloat16 [256, 2048], P('tok', 'head'), may hold values from -6 to 6
- audio_k: bfloat16 [256, 2048], P('tok', 'head'), may hold values from -6 to 6
- audio_v: bfloat16 [256, 2048], P('tok', 'head'), may hold values from -6 to 6
- norm_gain: float32 [2048], replicated, may hold values from 0.5 to 1.5
Outputs:
- video_out: bfloat16 [7168, 2048], P(('tok', 'head'))
- audio_out: bfloat16 [256, 2048], P('tok', 'head')
All inputs are finite; a program needn't handle non-finite values.
Results may differ from a plain program's by a relative error of at most 0.0095.
Values may be sent and summed in bfloat16 or wider, within the bound.
No kernel may reach another device: no remote copies, remote signals or barrier semaphores. Data moves between devices by JAX's collectives and lax.ppermute only.
A program may use at most 64 MiB of HBM per device.

v0:
```python
import jax
import jax.numpy as jnp
from jax import lax
from jax.sharding import PartitionSpec as P

HEAD_DIM = 64


def shards(video_q, video_k, video_v, audio_q, audio_k, audio_v, norm_gain):
    query_rows, local_width = video_q.shape
    heads_here = local_width // HEAD_DIM
    audio_rows = audio_q.shape[0]
    scaling = HEAD_DIM ** (-0.5)

    def split_heads(matrix):
        return matrix.reshape(matrix.shape[0], heads_here, HEAD_DIM)

    video_heads = split_heads(video_q)
    pieces = (
        lax.all_gather(audio_k, "tok", axis=0, tiled=True),
        lax.all_gather(audio_v, "tok", axis=0, tiled=True),
    )
    running_max = jnp.full((heads_here, query_rows), -1e30, jnp.float32)
    running_sum = jnp.zeros((heads_here, query_rows), jnp.float32)
    running_out = jnp.zeros((heads_here, query_rows, HEAD_DIM), jnp.float32)
    key_block = split_heads(pieces[0])
    value_block = split_heads(pieces[1])
    max_list = []
    sum_list = []
    out_list = []
    for absorb_head_index in range(heads_here):
        absorb_scores = (
            jnp.einsum(
                "qd,kd->qk",
                video_heads[:, absorb_head_index],
                key_block[:, absorb_head_index],
                preferred_element_type=jnp.float32,
            )
            * scaling
        )
        new_max = jnp.maximum(running_max[absorb_head_index], jnp.max(absorb_scores, axis=1))
        absorb_weights = jnp.exp(absorb_scores - new_max[:, None])
        factor = jnp.exp(running_max[absorb_head_index] - new_max)
        sum_list.append(running_sum[absorb_head_index] * factor + jnp.sum(absorb_weights, axis=1))
        out_list.append(
            running_out[absorb_head_index] * factor[:, None]
            + jnp.dot(
                absorb_weights.astype(jnp.bfloat16),
                value_block[:, absorb_head_index],
                preferred_element_type=jnp.float32,
            )
        )
        max_list.append(new_max)
    final_sum = jnp.stack(sum_list)
    final_out = jnp.stack(out_list)
    video_attn = (
        (final_out / final_sum[:, :, None]).transpose(1, 0, 2).reshape(query_rows, local_width)
    )
    video_attn = video_attn.astype(jnp.bfloat16)
    head_count = lax.axis_size("head")
    pieces = video_attn.reshape(head_count, query_rows // head_count, local_width)
    received = lax.all_to_all(pieces, "head", split_axis=0, concat_axis=2, tiled=True)
    normalize_received = received[0]
    widened = normalize_received.astype(jnp.float32)
    mean_square = jnp.mean(widened * widened, axis=-1, keepdims=True)
    video_out = (widened * lax.rsqrt(mean_square + 1e-06) * norm_gain).astype(jnp.bfloat16)
    all_queries = split_heads(lax.all_gather(audio_q, "tok", axis=0, tiled=True))
    video_keys = split_heads(video_k)
    video_values = split_heads(video_v)
    max_list, sum_list, out_list = ([], [], [])
    for head_index in range(heads_here):
        scores = (
            jnp.einsum(
                "qd,kd->qk",
                all_queries[:, head_index],
                video_keys[:, head_index],
                preferred_element_type=jnp.float32,
            )
            * scaling
        )
        local_max = jnp.max(scores, axis=1)
        weights = jnp.exp(scores - local_max[:, None])
        max_list.append(local_max)
        sum_list.append(jnp.sum(weights, axis=1))
        out_list.append(
            jnp.dot(
                weights.astype(jnp.bfloat16),
                video_values[:, head_index],
                preferred_element_type=jnp.float32,
            )
        )
    part_max = jnp.stack(max_list)
    part_sum = jnp.stack(sum_list)
    part_out = jnp.stack(out_list)
    tok_count = lax.axis_size("tok")
    grouped_max = part_max.reshape(heads_here, tok_count, audio_rows)
    grouped_sum = part_sum.reshape(heads_here, tok_count, audio_rows)
    grouped_out = part_out.reshape(heads_here, tok_count, audio_rows, HEAD_DIM)
    got_max, got_sum, got_out = (
        lax.all_to_all(grouped_max, "tok", split_axis=1, concat_axis=1, tiled=True),
        lax.all_to_all(grouped_sum, "tok", split_axis=1, concat_axis=1, tiled=True),
        lax.all_to_all(grouped_out, "tok", split_axis=1, concat_axis=1, tiled=True),
    )
    joint_max = jnp.max(got_max, axis=1, keepdims=True)
    factor = jnp.exp(got_max - joint_max)
    own_sum = jnp.sum(got_sum * factor, axis=1)
    own_out = jnp.sum(got_out * factor[:, :, :, None], axis=1)
    audio_out = (own_out / own_sum[:, :, None]).transpose(1, 0, 2).reshape(audio_rows, local_width)
    return (video_out, audio_out.astype(jnp.bfloat16))


def solution(mesh):
    placed = (
        P("tok", "head"),
        P("tok", "head"),
        P("tok", "head"),
        P("tok", "head"),
        P("tok", "head"),
        P("tok", "head"),
        P(),
    )
    return jax.shard_map(
        shards,
        mesh=mesh,
        in_specs=placed,
        out_specs=(P(("tok", "head"), None), P("tok", "head")),
        check_vma=False,
    )
```

profile of v0, /device:TPU:2, one launch (start us, length us, event | category | flops | bytes accessed | tf_op | source)
XLA Modules:
  0.0 136.5 jit_solution(5439281923956498559)
XLA Ops:
  0.6 1.5 %copy.41 = bf16[896,512]{0,1:T(8,128)(2,1)S(1)} copy(bf16[896,512]{1,0:T(8,128)(2,1)} %param.8) | data formatting | bytes 1835008 | tf_op args[1]
  2.2 9.3 %all_gather.11 = bf16[256,512]{1,0:T(8,128)(2,1)S(1)} all-gather(bf16[32,512]{1,0:T(8,128)(2,1)S(1)} %copy-done.27), channel_id=1, replica_groups=mesh['head'=4,'tok'=8] {'tok'}, dimensions={0}, use_global_device_ids=true | all-gather | bytes 294912 | tf_op jit(solution)/shard_map/all_gather | solution.py:67
  11.6 1.3 fusion.91
  12.9 1.2 fusion.92
  14.2 1.3 fusion.93
  15.5 1.2 fusion.94
  16.7 1.3 fusion.95
  18.0 1.3 fusion.96
  19.2 1.2 fusion.97
  20.5 1.2 fusion.98
  23.2 3.8 %all-to-all-start.2 = ((f32[8,1,256]{2,1,0:T(1,128)}), f32[8,1,256]{2,1,0:T(1,128)S(1)}, u32[]{:S(2)}, u32[]{:S(2)}) async-start(f32[8,1,256]{2,1,0:T(1,128)} %reshape.485), calls=%async_computation.2 | async-start | bytes 16384 | tf_op jit(solution)/shard_map/all_to_all | solution.py:100
  26.9 9.3 %all_gather.9 = bf16[256,512]{1,0:T(8,128)(2,1)S(1)} all-gather(bf16[32,512]{1,0:T(8,128)(2,1)S(1)} %copy-done.28), channel_id=1, replica_groups=mesh['head'=4,'tok'=8] {'tok'}, dimensions={0}, use_global_device_ids=true | all-gather | bytes 294912 | tf_op jit(solution)/shard_map/all_gather | solution.py:20
  37.4 1.3 fusion.84
  38.6 1.3 fusion.85
  39.9 1.3 fusion.86
  41.2 1.3 fusion.87
  43.1 1.2 fusion.90
  44.6 8.5 %all_gather.10 = bf16[256,512]{1,0:T(8,128)(2,1)S(1)} all-gather(bf16[32,512]{1,0:T(8,128)(2,1)S(1)} %copy-done.29), channel_id=1, replica_groups=mesh['head'=4,'tok'=8] {'tok'}, dimensions={0}, use_global_device_ids=true | all-gather | bytes 294912 | tf_op jit(solution)/shard_map/all_gather | solution.py:21
  53.3 1.5 %fusion.28 = f32[896]{0:T(1024)S(1)} fusion(f32[896,256]{0,1:T(8,128)} %get-tuple-element.39, f32[896]{0:T(1024)S(1)} %broadcast_maximum_fusion.6), kind=kLoop, calls=%fused_computation.81 | loop fusion | flops 457856 | bytes 924672 | tf_op jit(solution)/shard_map/reduce_sum | solution.py:44
  54.7 1.3 fusion.30
  59.8 0.8 fusion.42
  60.6 1.6 %fusion.44 = (f32[256]{0:T(256)}, bf16[256,896]{1,0:T(8,128)(2,1)}) fusion(f32[256,896]{1,0:T(8,128)S(1)} %copy-done.13, f32[256]{0:T(256)S(1)} %copy-done.48), kind=kLoop, calls=%fused_computation.97 | loop fusion | flops 687872 | bytes 1378304 | tf_op jit(solution)/shard_map/reduce_sum | solution.py:84
  62.2 1.6 %fusion.46 = (f32[256]{0:T(256)}, bf16[256,896]{1,0:T(8,128)(2,1)}) fusion(f32[256,896]{1,0:T(8,128)S(1)} %copy-done.12, f32[256]{0:T(256)S(1)} %copy-done.46), kind=kLoop, calls=%fused_computation.99 | loop fusion | flops 687872 | bytes 1378304 | tf_op jit(solution)/shard_map/reduce_sum | solution.py:84
  63.8 1.6 %fusion.48 = (f32[256]{0:T(256)}, bf16[256,896]{1,0:T(8,128)(2,1)}) fusion(f32[256,896]{1,0:T(8,128)S(1)} %copy-done.11, f32[256]{0:T(256)S(1)} %copy-done.44), kind=kLoop, calls=%fused_computation.101 | loop fusion | flops 687872 | bytes 1378304 | tf_op jit(solution)/shard_map/reduce_sum | solution.py:84
  65.4 1.5 %fusion.50 = (f32[256]{0:T(256)}, bf16[256,896]{1,0:T(8,128)(2,1)}) fusion(f32[256,896]{1,0:T(8,128)S(1)} %copy-done.10, f32[256]{0:T(256)S(1)} %copy-done.42), kind=kLoop, calls=%fused_computation.103 | loop fusion | flops 687872 | bytes 1378304 | tf_op jit(solution)/shard_map/reduce_sum | solution.py:84
  67.0 1.6 %fusion.52 = (f32[256]{0:T(256)}, bf16[256,896]{1,0:T(8,128)(2,1)}) fusion(f32[256,896]{1,0:T(8,128)S(1)} %copy-done.9, f32[256]{0:T(256)S(1)} %copy-done.40), kind=kLoop, calls=%fused_computation.105 | loop fusion | flops 687872 | bytes 1378304 | tf_op jit(solution)/shard_map/reduce_sum | solution.py:84
  68.6 1.6 %fusion.54 = (f32[256]{0:T(256)}, bf16[256,896]{1,0:T(8,128)(2,1)}) fusion(f32[256,896]{1,0:T(8,128)S(1)} %copy-done.8, f32[256]{0:T(256)S(1)} %copy-done.38), kind=kLoop, calls=%fused_computation.107 | loop fusion | flops 687872 | bytes 1378304 | tf_op jit(solution)/shard_map/reduce_sum | solution.py:84
  70.2 1.5 %fusion.56 = (f32[256]{0:T(256)}, bf16[256,896]{1,0:T(8,128)(2,1)}) fusion(f32[256,896]{1,0:T(8,128)S(1)} %copy-done.7, f32[256]{0:T(256)S(1)} %copy-done.36), kind=kLoop, calls=%fused_computation.109 | loop fusion | flops 687872 | bytes 1378304 | tf_op jit(solution)/shard_map/reduce_sum | solution.py:84
  71.7 2.2 %copy.42 = bf16[896,512]{0,1:T(8,128)(2,1)} copy(bf16[896,512]{1,0:T(8,128)(2,1)} %param.9) | data formatting | bytes 1835008 | tf_op args[2]
  73.9 1.6 %fusion.16 = f32[8,896,64]{1,2,0:T(8,128)S(1)} fusion(f32[896,256]{0,1:T(8,128)} %copy-done.5, f32[896]{0:T(1024)S(1)} %broadcast_maximum_fusion.7, f32[896]{0:T(1024)S(1)} %get-tuple-element.35, bf16[256,8,64]{0,2,1:T(8,128)(2,1)S(1)} %bitcast.365), kind=kOutput, calls=%fused_computation.44 | convolution fusion | flops 29876224 | bytes 1187840 | tf_op jit(solution)/shard_map/dot_general | solution.py:47
  75.5 1.5 %fusion.14 = f32[8,896,64]{1,2,0:T(8,128)S(1)} fusion(f32[8,896,64]{1,2,0:T(8,128)S(1)} %fusion.16, f32[896,256]{0,1:T(8,128)} %get-tuple-element.39, f32[896]{0:T(1024)S(1)} %broadcast_maximum_fusion.6, f32[896]{0:T(1024)S(1)} %get-tuple-element.33, bf16[256,8,64]{0,2,1:T(8,128)(2,1)S(1)} %bitcast.366), kind=kOutput, calls=%fused_computation.41 | convolution fusion | flops 29876224 | bytes 1187840 | tf_op jit(solution)/shard_map/dot_general | solution.py:47
  81.2 1.0 copy-done.24
  83.7 4.7 %all-to-all-start.3 = ((f32[8,1,256]{2,1,0:T(1,128)}), f32[8,1,256]{2,1,0:T(1,128)S(1)}, u32[]{:S(2)}, u32[]{:S(2)}) async-start(f32[8,1,256]{2,1,0:T(1,128)} %reshape.487), calls=%async_computation.3 | async-start | bytes 16384 | tf_op jit(solution)/shard_map/all_to_all | solution.py:101
  88.7 1.5 %reshape.483 = f32[8,1,16384]{2,1,0:T(1,128)} reshape(f32[8,8,32,64]{3,2,1,0:T(8,128)S(1)} %bitcast.332) | data formatting | bytes 1048576
  90.2 1.5 %all-to-all-done.3 = f32[8,1,256]{2,1,0:T(1,128)S(1)} async-done(((f32[8,1,256]{2,1,0:T(1,128)}), f32[8,1,256]{2,1,0:T(1,128)S(1)}, u32[]{:S(2)}, u32[]{:S(2)}) %all-to-all-start.3) | async-done | bytes 8224 | tf_op jit(solution)/shard_map/all_to_all | solution.py:101
  91.7 4.9 %all-to-all-start.1 = ((f32[8,1,16384]{2,1,0:T(1,128)}), f32[8,1,16384]{2,1,0:T(1,128)S(1)}, u32[]{:S(2)}, u32[]{:S(2)}) async-start(f32[8,1,16384]{2,1,0:T(1,128)} %reshape.483), calls=%async_computation.1 | async-start | bytes 1048576 | tf_op jit(solution)/shard_map/all_to_all | solution.py:102
  96.6 1.0 fusion.2
  97.6 1.7 %fusion.25 = bf16[896,8,64]{0,2,1:T(8,128)(2,1)S(1)} fusion(f32[8,896,64]{1,2,0:T(8,128)} %fusion.2, f32[8,896]{1,0:T(8,128)S(1)} %stack.112), kind=kLoop, calls=%fused_computation.78 | loop fusion | flops 917504 | bytes 2781184 | tf_op jit(solution)/shard_map/convert_element_type | solution.py:59
  99.2 0.9 convert_element_type.94
  100.1 1.4 %copy.38 = bf16[4,224,512]{2,1,0:T(8,128)(2,1)} copy(bf16[4,224,512]{1,0,2:T(4,128)(2,1)S(1)} %convert_element_type.94) | data formatting | bytes 1835008 | tf_op jit(solution)/shard_map/convert_element_type | solution.py:59
  101.5 3.4 %all-to-all-done.1 = f32[8,1,16384]{2,1,0:T(1,128)S(1)} async-done(((f32[8,1,16384]{2,1,0:T(1,128)}), f32[8,1,16384]{2,1,0:T(1,128)S(1)}, u32[]{:S(2)}, u32[]{:S(2)}) %all-to-all-start.1) | async-done | bytes 524320 | tf_op jit(solution)/shard_map/all_to_all | solution.py:102
  104.9 4.9 %all-to-all-start = ((bf16[4,224,512]{2,1,0:T(8,128)(2,1)}), bf16[4,224,512]{2,1,0:T(8,128)(2,1)S(1)}, u32[]{:S(2)}, u32[]{:S(2)}) async-start(bf16[4,224,512]{2,1,0:T(8,128)(2,1)} %copy.38), calls=%async_computation | async-start | bytes 1835008 | tf_op jit(solution)/shard_map/all_to_all | solution.py:62
  111.8 1.9 %reduce.5 = f32[8,16384]{1,0:T(8,128)S(1)} reduce(f32[8,1,16384]{2,1,0:T(1,128)S(1)} %all-to-all-done.1, f32[]{:T(128)} %broadcast.428), dimensions={1}, to_apply=%all_to_all.17.reduce_sub_computation | reduce | bytes 1048580 | tf_op jit(solution)/shard_map/all_to_all | solution.py:102
  114.6 0.7 convert_element_type.110
  115.3 17.6 %all-to-all-done = bf16[4,224,512]{2,1,0:T(8,128)(2,1)S(1)} async-done(((bf16[4,224,512]{2,1,0:T(8,128)(2,1)}), bf16[4,224,512]{2,1,0:T(8,128)(2,1)S(1)}, u32[]{:S(2)}, u32[]{:S(2)}) %all-to-all-start) | async-done | bytes 917536 | tf_op jit(solution)/shard_map/all_to_all | solution.py:62
  133.1 1.2 copy.39
  134.3 0.7 copy.49
  135.4 1.1 multiply_convert_fusion
  (206 shorter events, 16.4 us)
Async XLA Ops:
  12.9 8.8 %copy-start.49 = (f32[256]{0:T(256)}, f32[256]{0:T(256)S(1)}, u32[]{:S(2)}) copy-start(f32[256]{0:T(256)S(1)} %get-tuple-element.52) | copy-start | bytes 3076
  14.2 7.7 %copy-start.47 = (f32[256]{0:T(256)}, f32[256]{0:T(256)S(1)}, u32[]{:S(2)}) copy-start(f32[256]{0:T(256)S(1)} %get-tuple-element.54) | copy-start | bytes 3076
  15.5 6.4 %copy-start.45 = (f32[256]{0:T(256)}, f32[256]{0:T(256)S(1)}, u32[]{:S(2)}) copy-start(f32[256]{0:T(256)S(1)} %get-tuple-element.56) | copy-start | bytes 3076
  16.7 5.3 %copy-start.43 = (f32[256]{0:T(256)}, f32[256]{0:T(256)S(1)}, u32[]{:S(2)}) copy-start(f32[256]{0:T(256)S(1)} %get-tuple-element.58) | copy-start | bytes 3076
  18.0 18.2 %copy-start.41 = (f32[256]{0:T(256)}, f32[256]{0:T(256)S(1)}, u32[]{:S(2)}) copy-start(f32[256]{0:T(256)S(1)} %get-tuple-element.60) | copy-start | bytes 3076
  18.0 9.0 %copy-start.28 = (bf16[32,512]{1,0:T(8,128)(2,1)S(1)}, bf16[32,512]{1,0:T(8,128)(2,1)}, u32[]{:S(2)}) copy-start(bf16[32,512]{1,0:T(8,128)(2,1)} %param.11) | copy-start | bytes 98308
  18.0 18.4 %copy-start.26 = (bf16[896,512]{1,0:T(8,128)(2,1)S(1)}, bf16[896,512]{1,0:T(8,128)(2,1)}, u32[]{:S(2)}) copy-start(bf16[896,512]{1,0:T(8,128)(2,1)} %param.7) | copy-start | bytes 2752516
  19.2 17.7 %copy-start.39 = (f32[256]{0:T(256)}, f32[256]{0:T(256)S(1)}, u32[]{:S(2)}) copy-start(f32[256]{0:T(256)S(1)} %get-tuple-element.62) | copy-start | bytes 3076
  20.5 16.5 %copy-start.37 = (f32[256]{0:T(256)}, f32[256]{0:T(256)S(1)}, u32[]{:S(2)}) copy-start(f32[256]{0:T(256)S(1)} %get-tuple-element.64) | copy-start | bytes 3076
  21.7 15.6 %copy-start.35 = (f32[256]{0:T(256)}, f32[256]{0:T(256)S(1)}, u32[]{:S(2)}) copy-start(f32[256]{0:T(256)S(1)} %get-tuple-element.66) | copy-start | bytes 3076
  23.2 60.6 %all-to-all-start.2 = ((f32[8,1,256]{2,1,0:T(1,128)}), f32[8,1,256]{2,1,0:T(1,128)S(1)}, u32[]{:S(2)}, u32[]{:S(2)}) async-start(f32[8,1,256]{2,1,0:T(1,128)} %reshape.485), calls=%async_computation.2 | async-start | bytes 16384 | tf_op jit(solution)/shard_map/all_to_all | solution.py:100
  37.0 5.8 %copy-start.6 = (bf16[896,512]{0,1:T(8,128)(2,1)}, bf16[896,512]{0,1:T(8,128)(2,1)S(1)}, u32[]{:S(2)}) copy-start(bf16[896,512]{0,1:T(8,128)(2,1)S(1)} %copy.35) | copy-start | bytes 2752516
  37.3 7.0 %copy-start.5 = (f32[896,256]{0,1:T(8,128)}, f32[896,256]{0,1:T(8,128)S(1)}, u32[]{:S(2)}) copy-start(f32[896,256]{0,1:T(8,128)S(1)} %get-tuple-element.37) | copy-start | bytes 2752516
  53.2 3.4 %copy-start.2 = (f32[896,256]{0,1:T(8,128)S(1)}, f32[896,256]{0,1:T(8,128)}, u32[]{:S(2)}) copy-start(f32[896,256]{0,1:T(8,128)} %get-tuple-element.43) | copy-start | bytes 2752516
  53.2 4.2 %copy-start = (f32[896,256]{0,1:T(8,128)S(1)}, f32[896,256]{0,1:T(8,128)}, u32[]{:S(2)}) copy-start(f32[896,256]{0,1:T(8,128)} %get-tuple-element.45) | copy-start | bytes 2752516
  56.7 3.1 %copy-start.14 = (f32[256,896]{1,0:T(8,128)S(1)}, f32[256,896]{1,0:T(8,128)}, u32[]{:S(2)}) copy-start(f32[256,896]{1,0:T(8,128)} %get-tuple-element.53) | copy-start | bytes 2752516
  56.7 3.1 %copy-start.50 = (f32[256]{0:T(256)S(1)}, f32[256]{0:T(256)}, u32[]{:S(2)}) copy-start(f32[256]{0:T(256)} %copy-done.49) | copy-start | bytes 3076
  57.6 3.0 %copy-start.13 = (f32[256,896]{1,0:T(8,128)S(1)}, f32[256,896]{1,0:T(8,128)}, u32[]{:S(2)}) copy-start(f32[256,896]{1,0:T(8,128)} %get-tuple-element.55) | copy-start | bytes 2752516
  57.6 3.0 %copy-start.48 = (f32[256]{0:T(256)S(1)}, f32[256]{0:T(256)}, u32[]{:S(2)}) copy-start(f32[256]{0:T(256)} %copy-done.47) | copy-start | bytes 3076
  59.0 3.2 %copy-start.12 = (f32[256,896]{1,0:T(8,128)S(1)}, f32[256,896]{1,0:T(8,128)}, u32[]{:S(2)}) copy-start(f32[256,896]{1,0:T(8,128)} %get-tuple-element.57) | copy-start | bytes 2752516
  59.0 3.2 %copy-start.46 = (f32[256]{0:T(256)S(1)}, f32[256]{0:T(256)}, u32[]{:S(2)}) copy-start(f32[256]{0:T(256)} %copy-done.45) | copy-start | bytes 3076
  59.8 4.1 %copy-start.11 = (f32[256,896]{1,0:T(8,128)S(1)}, f32[256,896]{1,0:T(8,128)}, u32[]{:S(2)}) copy-start(f32[256,896]{1,0:T(8,128)} %get-tuple-element.59) | copy-start | bytes 2752516
  59.8 4.1 %copy-start.44 = (f32[256]{0:T(256)S(1)}, f32[256]{0:T(256)}, u32[]{:S(2)}) copy-start(f32[256]{0:T(256)} %copy-done.43) | copy-start | bytes 3076
  60.6 4.8 %copy-start.10 = (f32[256,896]{1,0:T(8,128)S(1)}, f32[256,896]{1,0:T(8,128)}, u32[]{:S(2)}) copy-start(f32[256,896]{1,0:T(8,128)} %get-tuple-element.61) | copy-start | bytes 2752516
  60.6 4.8 %copy-start.42 = (f32[256]{0:T(256)S(1)}, f32[256]{0:T(256)}, u32[]{:S(2)}) copy-start(f32[256]{0:T(256)} %copy-done.41) | copy-start | bytes 3076
  62.2 4.8 %copy-start.9 = (f32[256,896]{1,0:T(8,128)S(1)}, f32[256,896]{1,0:T(8,128)}, u32[]{:S(2)}) copy-start(f32[256,896]{1,0:T(8,128)} %get-tuple-element.63) | copy-start | bytes 2752516
  62.2 4.8 %copy-start.40 = (f32[256]{0:T(256)S(1)}, f32[256]{0:T(256)}, u32[]{:S(2)}) copy-start(f32[256]{0:T(256)} %copy-done.39) | copy-start | bytes 3076
  63.8 4.8 %copy-start.8 = (f32[256,896]{1,0:T(8,128)S(1)}, f32[256,896]{1,0:T(8,128)}, u32[]{:S(2)}) copy-start(f32[256,896]{1,0:T(8,128)} %get-tuple-element.65) | copy-start | bytes 2752516
  63.8 4.8 %copy-start.38 = (f32[256]{0:T(256)S(1)}, f32[256]{0:T(256)}, u32[]{:S(2)}) copy-start(f32[256]{0:T(256)} %copy-done.37) | copy-start | bytes 3076
  65.4 4.7 %copy-start.7 = (f32[256,896]{1,0:T(8,128)S(1)}, f32[256,896]{1,0:T(8,128)}, u32[]{:S(2)}) copy-start(f32[256,896]{1,0:T(8,128)} %get-tuple-element.67) | copy-start | bytes 2752516
  65.4 4.7 %copy-start.36 = (f32[256]{0:T(256)S(1)}, f32[256]{0:T(256)}, u32[]{:S(2)}) copy-start(f32[256]{0:T(256)} %copy-done.35) | copy-start | bytes 3076
  73.9 3.1 %copy-start.4 = (f32[896,256]{0,1:T(8,128)S(1)}, f32[896,256]{0,1:T(8,128)}, u32[]{:S(2)}) copy-start(f32[896,256]{0,1:T(8,128)} %get-tuple-element.41) | copy-start | bytes 2752516
  73.9 3.4 %copy-start.3 = (f32[896,256]{0,1:T(8,128)S(1)}, f32[896,256]{0,1:T(8,128)}, u32[]{:S(2)}) copy-start(f32[896,256]{0,1:T(8,128)} %get-tuple-element.43) | copy-start | bytes 2752516
  79.9 2.6 %copy-start.54 = (f32[256]{0:T(256)S(1)}, f32[256]{0:T(256)}, u32[]{:S(2)}) copy-start(f32[256]{0:T(256)} %get-tuple-element.14) | copy-start | bytes 3076
  79.9 2.6 %copy-start.55 = (f32[256]{0:T(256)S(1)}, f32[256]{0:T(256)}, u32[]{:S(2)}) copy-start(f32[256]{0:T(256)} %get-tuple-element.12) | copy-start | bytes 3076
  79.9 2.7 %copy-start.56 = (f32[256]{0:T(256)S(1)}, f32[256]{0:T(256)}, u32[]{:S(2)}) copy-start(f32[256]{0:T(256)} %get-tuple-element.10) | copy-start | bytes 3076
  79.9 2.8 %copy-start.57 = (f32[256]{0:T(256)S(1)}, f32[256]{0:T(256)}, u32[]{:S(2)}) copy-start(f32[256]{0:T(256)} %get-tuple-element.8) | copy-start | bytes 3076
  80.0 2.9 %copy-start.58 = (f32[256]{0:T(256)S(1)}, f32[256]{0:T(256)}, u32[]{:S(2)}) copy-start(f32[256]{0:T(256)} %get-tuple-element.6) | copy-start | bytes 3076
  80.0 2.9 %copy-start.59 = (f32[256]{0:T(256)S(1)}, f32[256]{0:T(256)}, u32[]{:S(2)}) copy-start(f32[256]{0:T(256)} %get-tuple-element.4) | copy-start | bytes 3076
  80.0 8.5 %copy-start.30 = (f32[896]{0:T(1024)S(1)}, f32[896]{0:T(1024)}, u32[]{:S(2)}) copy-start(f32[896]{0:T(1024)} %get-tuple-element.30) | copy-start | bytes 10756
  80.0 8.5 %copy-start.31 = (f32[896]{0:T(1024)S(1)}, f32[896]{0:T(1024)}, u32[]{:S(2)}) copy-start(f32[896]{0:T(1024)} %get-tuple-element.28) | copy-start | bytes 10756
  80.0 8.5 %copy-start.32 = (f32[896]{0:T(1024)S(1)}, f32[896]{0:T(1024)}, u32[]{:S(2)}) copy-start(f32[896]{0:T(1024)} %get-tuple-element.26) | copy-start | bytes 10756
  80.0 8.6 %copy-start.33 = (f32[896]{0:T(1024)S(1)}, f32[896]{0:T(1024)}, u32[]{:S(2)}) copy-start(f32[896]{0:T(1024)} %get-tuple-element.24) | copy-start | bytes 10756
  80.0 8.6 %copy-start.34 = (f32[896]{0:T(1024)S(1)}, f32[896]{0:T(1024)}, u32[]{:S(2)}) copy-start(f32[896]{0:T(1024)} %get-tuple-element.22) | copy-start | bytes 10756
  82.1 6.5 %copy-start.25 = (f32[8,8,32,64]{3,2,1,0:T(8,128)S(1)}, f32[8,8,32,64]{3,2,1,0:T(8,128)}, u32[]{:S(2)}) copy-start(f32[8,8,32,64]{3,2,1,0:T(8,128)} %copy-done.24) | copy-start | bytes 1572868
  83.7 8.0 %all-to-all-start.3 = ((f32[8,1,256]{2,1,0:T(1,128)}), f32[8,1,256]{2,1,0:T(1,128)S(1)}, u32[]{:S(2)}, u32[]{:S(2)}) async-start(f32[8,1,256]{2,1,0:T(1,128)} %reshape.487), calls=%async_computation.3 | async-start | bytes 16384 | tf_op jit(solution)/shard_map/all_to_all | solution.py:101
  91.7 13.1 %all-to-all-start.1 = ((f32[8,1,16384]{2,1,0:T(1,128)}), f32[8,1,16384]{2,1,0:T(1,128)S(1)}, u32[]{:S(2)}, u32[]{:S(2)}) async-start(f32[8,1,16384]{2,1,0:T(1,128)} %reshape.483), calls=%async_computation.1 | async-start | bytes 1048576 | tf_op jit(solution)/shard_map/all_to_all | solution.py:102
  104.9 28.0 %all-to-all-start = ((bf16[4,224,512]{2,1,0:T(8,128)(2,1)}), bf16[4,224,512]{2,1,0:T(8,128)(2,1)S(1)}, u32[]{:S(2)}, u32[]{:S(2)}) async-start(bf16[4,224,512]{2,1,0:T(8,128)(2,1)} %copy.38), calls=%async_computation | async-start | bytes 1835008 | tf_op jit(solution)/shard_map/all_to_all | solution.py:62
  (16 other events, 26.8 us)
where the time goes:
time: 137 us
  blocking collectives  27.1 us (20%)
  other arithmetic  25.6 us (19%)
  matrix products  24.9 us (18%)
  waiting for transfers between devices  22.4 us (16%)
  starting transfers between devices  18.2 us (13%)
  local copies, waits for them, and re-layouts  16.8 us (12%)
  between operations  1.52 us (1%)
    all_to_all x1, waiting for transfers between devices, shards(): lax.all_to_all(pieces, 'head', split_axis=0, concat_axis=2, tiled=True)  17.6 us
    reduce_sum x8, other arithmetic, shards(): sum_list.append(jnp.sum(weights, axis=1))  11.8 us
    dot_general x8, matrix products, shards(): jnp.einsum('qd,kd->qk', all_queries[:, head_index], video_keys[:, head_in...  10.1 us
    unnamed x130, local copies, waits for them, and re-layouts  10 us
    all_gather x1, blocking collectives, shards(): lax.all_gather(audio_q, 'tok', axis=0, tiled=True)  9.31 us
    all_gather x1, blocking collectives, shards(): lax.all_gather(audio_k, 'tok', axis=0, tiled=True)  9.26 us
    all_gather x1, blocking collectives, shards(): lax.all_gather(audio_v, 'tok', axis=0, tiled=True)  8.52 us
    dot_general x8, matrix products, shards(): jnp.einsum('qd,kd->qk', video_heads[:, absorb_head_index], key_block[:, a...  7.34 us
  transfers between devices with their start and end apart: 4, of which 3 were waited for; matrix products, arithmetic and copies ran while one was open for 36% of the time, Pallas kernels for 0%

commit v1 on v0

--- a/solution.py
+++ b/solution.py
@@ -4,6 +4,22 @@
 from jax.sharding import PartitionSpec as P
 
 HEAD_DIM = 64
+
+
+def collect(x, axis, dim):
+    ways, here, step = (lax.axis_size(axis), lax.axis_index(axis), x.shape[dim])
+    dims = [n * ways if d == dim else n for d, n in enumerate(x.shape)]
+    full = lax.dynamic_update_slice_in_dim(jnp.zeros(dims, x.dtype), x, here * step, axis=dim)
+    going_up = going_down = x
+    for far in range(1, ways // 2 + 1):
+        going_up = lax.ppermute(going_up, axis, [(d, (d + 1) % ways) for d in range(ways)])
+        full = lax.dynamic_update_slice_in_dim(full, going_up, (here - far) % ways * step, axis=dim)
+        if 2 * far < ways:
+            going_down = lax.ppermute(going_down, axis, [(d, (d - 1) % ways) for d in range(ways)])
+            full = lax.dynamic_update_slice_in_dim(
+                full, going_down, (here + far) % ways * step, axis=dim
+            )
+    return full
 
 
 def shards(video_q, video_k, video_v, audio_q, audio_k, audio_v, norm_gain):
@@ -16,10 +32,7 @@
         return matrix.reshape(matrix.shape[0], heads_here, HEAD_DIM)
 
     video_heads = split_heads(video_q)
-    pieces = (
-        lax.all_gather(audio_k, "tok", axis=0, tiled=True),
-        lax.all_gather(audio_v, "tok", axis=0, tiled=True),
-    )
+    pieces = (lax.all_gather(audio_k, "tok", axis=0, tiled=True), collect(audio_v, "tok", 0))
     running_max = jnp.full((heads_here, query_rows), -1e30, jnp.float32)
     running_sum = jnp.zeros((heads_here, query_rows), jnp.float32)
     running_out = jnp.zeros((heads_here, query_rows, HEAD_DIM), jnp.float32)

time: 137 us -> 165 us (1.20)
  local copies, waits for them, and re-layouts: 16.8 us -> 35.9 us
  starting transfers between devices: 18.2 us -> 28.2 us
  blocking collectives: 27.1 us -> 18.6 us
  waiting for transfers between devices: 22.4 us -> 27.5 us
  matrix products: 24.9 us -> 28.2 us
    dynamic_update_slice x0 -> x8, local copies, waits for them, and re-layouts: none -> 9.18 us  [the longest x4 4.58 us: collect(): lax.dynamic_update_slice_in_dim(full, going_up, (here - far) % ways * ste...]
    all_gather x1 -> x0, blocking collectives: 8.52 us -> none  [shards(): lax.all_gather(audio_v, 'tok', axis=0, tiled=True)]
    ppermute x0 -> x7, starting transfers between devices: none -> 6.8 us  [the longest x3 4.96 us: collect(): lax.ppermute(going_down, axis, [(d, (d - 1) % ways) for d in range(ways)])]
    ppermute x0 -> x7, waiting for transfers between devices: none -> 5.04 us  [the longest x4 4.71 us: collect(): lax.ppermute(going_up, axis, [(d, (d + 1) % ways) for d in range(ways)])]
    dot_general x8, matrix products: 5.39 us -> 10.3 us  [shards(): jnp.dot(absorb_weights.astype(jnp.bfloat16), value_block[:, absorb_head_i...]
    add x8, local copies, waits for them, and re-layouts: 0.03 us -> 4.74 us  [shards(): running_sum[absorb_head_index] * factor + jnp.sum(absorb_weights, axis=1)]
    dot_general x8, matrix products: 7.34 us -> 3.59 us  [shards(): jnp.einsum('qd,kd->qk', video_heads[:, absorb_head_index], key_block[:, a...]
    reduce_sum x8, other arithmetic: 3.7 us -> 1.21 us  [shards(): jnp.sum(absorb_weights, axis=1)]
  transfers between devices with their start and end apart: 4 -> 11, of which waited for: 3 -> 6; matrix products, arithmetic and copies ran while one was open for 36% -> 50% of each run, Pallas kernels for 0% -> 0%
where the time goes in v1:
time: 165 us; the launch traced here: 164 us
  local copies, waits for them, and re-layouts  35.9 us (22%)
  starting transfers between devices  28.2 us (17%)
  matrix products  28.2 us (17%)
  waiting for transfers between devices  27.5 us (17%)
  other arithmetic  24.4 us (15%)
  blocking collectives  18.6 us (11%)
    all_to_all x1, waiting for transfers between devices, shards(): lax.all_to_all(pieces, 'head', split_axis=0, concat_axis=2, tiled=True)  16.9 us
    unnamed x141, local copies, waits for them, and re-layouts  11.8 us
    reduce_sum x8, other arithmetic, shards(): sum_list.append(jnp.sum(weights, axis=1))  10.6 us
    dot_general x8, matrix products, shards(): jnp.dot(absorb_weights.astype(jnp.bfloat16), value_block[:, absorb_head_i...  10.3 us
    dot_general x8, matrix products, shards(): jnp.einsum('qd,kd->qk', all_queries[:, head_index], video_keys[:, head_in...  10.1 us
    all_gather x1, blocking collectives, shards(): lax.all_gather(audio_q, 'tok', axis=0, tiled=True)  9.31 us
    all_gather x1, blocking collectives, shards(): lax.all_gather(audio_k, 'tok', axis=0, tiled=True)  9.26 us
    all_to_all x1, starting transfers between devices, shards(): lax.all_to_all(grouped_sum, 'tok', split_axis=1, concat_axis=1, tiled=True)  6.45 us
  transfers between devices with their start and end apart: 11, of which 6 were waited for; matrix products, arithmetic and copies ran while one was open for 50% of the time, Pallas kernels for 0%

profile of v1, /device:TPU:2, one launch (start us, length us, event | category | flops | bytes accessed | tf_op | source)
XLA Modules:
  0.0 164.3 jit_solution(8188500328700637177)
XLA Ops:
  1.6 1.7 %collective-permute-start.1 = (bf16[32,512]{0,1:T(8,128)(2,1)S(1)}, bf16[32,512]{0,1:T(8,128)(2,1)}, u32[]{:S(2)}, u32[]{:S(2)}) collective-permute-start(bf16[32,512]{0,1:T(8,128)(2,1)S(1)} %copy.43), channel_id=1, source_target_pairs={{0,7},{1,0},{2,1},{3,2},{4,3},{5,4},{6,5},{7,6},{8,15},{9,8},{10,9... | collective-permute-start | bytes 98312 | tf_op jit(solution)/shard_map/ppermute | solution.py:18
  3.3 1.5 copy.49
  4.9 9.3 %all_gather.7 = bf16[256,512]{1,0:T(8,128)(2,1)S(1)} all-gather(bf16[32,512]{1,0:T(8,128)(2,1)S(1)} %copy-done.40), channel_id=1, replica_groups=mesh['head'=4,'tok'=8] {'tok'}, dimensions={0}, use_global_device_ids=true | all-gather | bytes 294912 | tf_op jit(solution)/shard_map/all_gather | solution.py:80
  14.3 1.2 fusion.91
  15.6 1.2 fusion.92
  16.8 1.3 fusion.93
  18.1 1.3 fusion.94
  19.5 1.2 fusion.95
  20.7 1.3 fusion.96
  22.0 1.3 fusion.97
  23.2 1.2 fusion.98
  25.9 5.3 %all-to-all-start.2 = ((f32[8,1,256]{2,1,0:T(1,128)}), f32[8,1,256]{2,1,0:T(1,128)}, u32[]{:S(2)}, u32[]{:S(2)}) async-start(f32[8,1,256]{2,1,0:T(1,128)} %reshape.485), calls=%async_computation.2 | async-start | bytes 16384 | tf_op jit(solution)/shard_map/all_to_all | solution.py:113
  31.1 9.3 %all_gather.6 = bf16[256,512]{1,0:T(8,128)(2,1)S(1)} all-gather(bf16[32,512]{1,0:T(8,128)(2,1)S(1)} %copy-done.41), channel_id=1, replica_groups=mesh['head'=4,'tok'=8] {'tok'}, dimensions={0}, use_global_device_ids=true | all-gather | bytes 294912 | tf_op jit(solution)/shard_map/all_gather | solution.py:35
  43.6 1.2 fusion.90
  49.8 1.6 fusion.44
  51.4 1.6 fusion.46
  53.0 1.6 fusion.48
  54.5 1.5 fusion.50
  57.1 1.6 fusion.54
  58.6 1.5 fusion.56
  60.2 2.2 %copy.50 = bf16[896,512]{0,1:T(8,128)(2,1)} copy(bf16[896,512]{1,0:T(8,128)(2,1)} %param.9) | data formatting | bytes 1835008 | tf_op args[2]
  62.6 1.3 fusion.24
  63.9 1.4 fusion.23
  69.0 1.4 collective-permute-start.3
  70.4 2.6 %collective-permute-done.2 = bf16[32,512]{0,1:T(8,128)(2,1)S(1)} collective-permute-done((bf16[32,512]{0,1:T(8,128)(2,1)S(1)}, bf16[32,512]{0,1:T(8,128)(2,1)S(1)}, u32[]{:S(2)}, u32[]{:S(2)}) %collective-permute-start.2) | collective-permute-done | bytes 32800 | tf_op jit(solution)/shard_map/ppermute | solution.py:15
  73.5 1.8 %collective-permute-start.5 = (bf16[32,512]{0,1:T(8,128)(2,1)S(1)}, bf16[32,512]{0,1:T(8,128)(2,1)}, u32[]{:S(2)}, u32[]{:S(2)}) collective-permute-start(bf16[32,512]{0,1:T(8,128)(2,1)S(1)} %collective-permute-done.3), channel_id=1, source_target_pairs={{0,7},{1,0},{2,1},{3,2},{4,3},{5,4},{6,5},{7,6},{8,15},{9,8},{10,9... | collective-permute-start | bytes 98312 | tf_op jit(solution)/shard_map/ppermute | solution.py:18
  75.3 2.1 %collective-permute-done.4 = bf16[32,512]{0,1:T(8,128)(2,1)S(1)} collective-permute-done((bf16[32,512]{0,1:T(8,128)(2,1)S(1)}, bf16[32,512]{0,1:T(8,128)(2,1)S(1)}, u32[]{:S(2)}, u32[]{:S(2)}) %collective-permute-start.4) | collective-permute-done | bytes 32800 | tf_op jit(solution)/shard_map/ppermute | solution.py:15
  77.4 1.4 collective-permute-start.6
  85.6 2.3 %copy.59 = f32[8,8,32,64]{3,2,0,1:T(8,128)} copy(f32[8,8,32,64]{3,2,1,0:T(8,128)} %copy-done.24) | data formatting | bytes 1048576 | tf_op jit(solution)/shard_map/stack | solution.py:107
  87.9 2.7 %reshape.483 = f32[8,1,16384]{2,1,0:T(1,128)} reshape(f32[8,8,32,64]{3,2,1,0:T(8,128)} %bitcast.332) | data formatting | bytes 1048576
  91.6 1.4 stack.112
  93.0 1.6 dynamic_update_slice.25
  94.7 1.7 %dynamic_update_slice.26 = bf16[256,512]{0,1:T(8,128)(2,1)S(1)} dynamic-update-slice(bf16[256,512]{0,1:T(8,128)(2,1)S(1)} %dynamic_update_slice.25, bf16[32,512]{0,1:T(8,128)(2,1)} %collective-permute-done.1, s32[]{:T(128)S(6)} %select_n.59, s32[]{:T(128)} %constant.66.clone.1) | dynamic-update-slice | bytes 65540 | tf_op jit(solution)/shard_map/dynamic_update_slice | solution.py:19
  98.1 1.6 dynamic_update_slice.30
  99.8 1.6 dynamic_update_slice.31
  101.4 2.3 %fusion.16 = f32[8,896,64]{1,2,0:T(8,128)} fusion(f32[896,256]{0,1:T(8,128)} %copy-done.7, f32[896]{0:T(1024)S(1)} %broadcast_maximum_fusion.7, f32[896]{0:T(1024)S(1)} %copy-done.42, bf16[256,8,64]{0,2,1:T(8,128)(2,1)S(1)} %bitcast.381), kind=kOutput, calls=%fused_computation.44 | convolution fusion | flops 29876224 | bytes 1187840 | tf_op jit(solution)/shard_map/dot_general | solution.py:60
  103.7 2.2 %fusion.14 = f32[8,896,64]{1,2,0:T(8,128)} fusion(f32[8,896,64]{1,2,0:T(8,128)} %fusion.16, f32[896,256]{0,1:T(8,128)} %copy-done.6, f32[896]{0:T(1024)S(1)} %broadcast_maximum_fusion.6, f32[896]{0:T(1024)S(1)} %copy-done.43, bf16[256,8,64]{0,2,1:T(8,128)(2,1)S(1)} %bitcast.382), kind=kOutput, calls=%fused_computation.41 | convolution fusion | flops 29876224 | bytes 1187840 | tf_op jit(solution)/shard_map/dot_general | solution.py:60
  109.9 6.5 %all-to-all-start.3 = ((f32[8,1,256]{2,1,0:T(1,128)}), f32[8,1,256]{2,1,0:T(1,128)S(1)}, u32[]{:S(2)}, u32[]{:S(2)}) async-start(f32[8,1,256]{2,1,0:T(1,128)} %reshape.487), calls=%async_computation.3 | async-start | bytes 16384 | tf_op jit(solution)/shard_map/all_to_all | solution.py:114
  117.3 2.3 %all-to-all-done.3 = f32[8,1,256]{2,1,0:T(1,128)S(1)} async-done(((f32[8,1,256]{2,1,0:T(1,128)}), f32[8,1,256]{2,1,0:T(1,128)S(1)}, u32[]{:S(2)}, u32[]{:S(2)}) %all-to-all-start.3) | async-done | bytes 8224 | tf_op jit(solution)/shard_map/all_to_all | solution.py:114
  119.6 4.9 %all-to-all-start.1 = ((f32[8,1,16384]{2,1,0:T(1,128)}), f32[8,1,16384]{2,1,0:T(1,128)S(1)}, u32[]{:S(2)}, u32[]{:S(2)}) async-start(f32[8,1,16384]{2,1,0:T(1,128)} %reshape.483), calls=%async_computation.1 | async-start | bytes 1048576 | tf_op jit(solution)/shard_map/all_to_all | solution.py:115
  125.4 1.7 %fusion.25 = bf16[896,8,64]{0,2,1:T(8,128)(2,1)S(1)} fusion(f32[8,896,64]{1,2,0:T(8,128)} %fusion.2, f32[8,896]{1,0:T(8,128)S(1)} %copy-done.31), kind=kLoop, calls=%fused_computation.78 | loop fusion | flops 917504 | bytes 2781184 | tf_op jit(solution)/shard_map/convert_element_type | solution.py:72
  127.9 1.4 copy.46
  129.4 3.3 %all-to-all-done.1 = f32[8,1,16384]{2,1,0:T(1,128)S(1)} async-done(((f32[8,1,16384]{2,1,0:T(1,128)}), f32[8,1,16384]{2,1,0:T(1,128)S(1)}, u32[]{:S(2)}, u32[]{:S(2)}) %all-to-all-start.1) | async-done | bytes 524320 | tf_op jit(solution)/shard_map/all_to_all | solution.py:115
  132.7 4.9 %all-to-all-start = ((bf16[4,224,512]{2,1,0:T(8,128)(2,1)}), bf16[4,224,512]{2,1,0:T(8,128)(2,1)S(1)}, u32[]{:S(2)}, u32[]{:S(2)}) async-start(bf16[4,224,512]{2,1,0:T(8,128)(2,1)} %copy.46), calls=%async_computation | async-start | bytes 1835008 | tf_op jit(solution)/shard_map/all_to_all | solution.py:75
  138.1 1.4 reduce.3
  140.3 1.9 %reduce.5 = f32[8,16384]{1,0:T(8,128)S(1)} reduce(f32[8,1,16384]{2,1,0:T(1,128)S(1)} %all-to-all-done.1, f32[]{:T(128)} %broadcast.435), dimensions={1}, to_apply=%all_to_all.17.reduce_sub_computation | reduce | bytes 1048580 | tf_op jit(solution)/shard_map/all_to_all | solution.py:115
  143.8 16.9 %all-to-all-done = bf16[4,224,512]{2,1,0:T(8,128)(2,1)S(1)} async-done(((bf16[4,224,512]{2,1,0:T(8,128)(2,1)}), bf16[4,224,512]{2,1,0:T(8,128)(2,1)S(1)}, u32[]{:S(2)}, u32[]{:S(2)}) %all-to-all-start) | async-done | bytes 917536 | tf_op jit(solution)/shard_map/all_to_all | solution.py:75
  161.0 1.2 copy.47
  (238 shorter events, 37.2 us)
Async XLA Ops:
  0.6 4.2 %copy-start.40 = (bf16[32,512]{1,0:T(8,128)(2,1)S(1)}, bf16[32,512]{1,0:T(8,128)(2,1)}, u32[]{:S(2)}) copy-start(bf16[32,512]{1,0:T(8,128)(2,1)} %param.10) | copy-start | bytes 98308
  1.5 14.0 %copy-start.26 = (bf16[32,512]{0,1:T(8,128)(2,1)}, bf16[32,512]{0,1:T(8,128)(2,1)S(1)}, u32[]{:S(2)}) copy-start(bf16[32,512]{0,1:T(8,128)(2,1)S(1)} %copy.43) | copy-start | bytes 98308
  1.5 67.1 %collective-permute-start = (bf16[32,512]{0,1:T(8,128)(2,1)S(1)}, bf16[32,512]{0,1:T(8,128)(2,1)S(1)}, u32[]{:S(2)}, u32[]{:S(2)}) collective-permute-start(bf16[32,512]{0,1:T(8,128)(2,1)S(1)} %copy.43), channel_id=1, source_target_pairs={{0,1},{1,2},{2,3},{3,4},{4,5},{5,6},{6,7},{7,0},{8,9},{9,10},{10,1... | collective-permute-start | bytes 98312 | tf_op jit(solution)/shard_map/ppermute | solution.py:15
  1.6 67.4 %collective-permute-start.1 = (bf16[32,512]{0,1:T(8,128)(2,1)S(1)}, bf16[32,512]{0,1:T(8,128)(2,1)}, u32[]{:S(2)}, u32[]{:S(2)}) collective-permute-start(bf16[32,512]{0,1:T(8,128)(2,1)S(1)} %copy.43), channel_id=1, source_target_pairs={{0,7},{1,0},{2,1},{3,2},{4,3},{5,4},{6,5},{7,6},{8,15},{9,8},{10,9... | collective-permute-start | bytes 98312 | tf_op jit(solution)/shard_map/ppermute | solution.py:18
  15.6 8.9 %copy-start.56 = (f32[256]{0:T(256)}, f32[256]{0:T(256)S(1)}, u32[]{:S(2)}) copy-start(f32[256]{0:T(256)S(1)} %get-tuple-element.52) | copy-start | bytes 3076
  16.8 7.7 %copy-start.54 = (f32[256]{0:T(256)}, f32[256]{0:T(256)S(1)}, u32[]{:S(2)}) copy-start(f32[256]{0:T(256)S(1)} %get-tuple-element.54) | copy-start | bytes 3076
  18.1 6.5 %copy-start.52 = (f32[256]{0:T(256)}, f32[256]{0:T(256)S(1)}, u32[]{:S(2)}) copy-start(f32[256]{0:T(256)S(1)} %get-tuple-element.56) | copy-start | bytes 3076
  19.5 5.3 %copy-start.50 = (f32[256]{0:T(256)}, f32[256]{0:T(256)S(1)}, u32[]{:S(2)}) copy-start(f32[256]{0:T(256)S(1)} %get-tuple-element.58) | copy-start | bytes 3076
  20.7 10.4 %copy-start.41 = (bf16[32,512]{1,0:T(8,128)(2,1)S(1)}, bf16[32,512]{1,0:T(8,128)(2,1)}, u32[]{:S(2)}) copy-start(bf16[32,512]{1,0:T(8,128)(2,1)} %param.11) | copy-start | bytes 98308
  20.7 19.8 %copy-start.25 = (bf16[896,512]{1,0:T(8,128)(2,1)S(1)}, bf16[896,512]{1,0:T(8,128)(2,1)}, u32[]{:S(2)}) copy-start(bf16[896,512]{1,0:T(8,128)(2,1)} %param.7) | copy-start | bytes 2752516
  25.9 84.0 %all-to-all-start.2 = ((f32[8,1,256]{2,1,0:T(1,128)}), f32[8,1,256]{2,1,0:T(1,128)}, u32[]{:S(2)}, u32[]{:S(2)}) async-start(f32[8,1,256]{2,1,0:T(1,128)} %reshape.485), calls=%async_computation.2 | async-start | bytes 16384 | tf_op jit(solution)/shard_map/all_to_all | solution.py:113
  42.5 4.6 %copy-start.2 = (f32[896,256]{0,1:T(8,128)}, f32[896,256]{0,1:T(8,128)S(1)}, u32[]{:S(2)}) copy-start(f32[896,256]{0,1:T(8,128)S(1)} %get-tuple-element.43) | copy-start | bytes 2752516
  42.9 5.0 %copy-start = (f32[896,256]{0,1:T(8,128)}, f32[896,256]{0,1:T(8,128)S(1)}, u32[]{:S(2)}) copy-start(f32[896,256]{0,1:T(8,128)S(1)} %get-tuple-element.45) | copy-start | bytes 2752516
  49.8 4.7 %copy-start.12 = (f32[256,896]{1,0:T(8,128)S(1)}, f32[256,896]{1,0:T(8,128)}, u32[]{:S(2)}) copy-start(f32[256,896]{1,0:T(8,128)} %get-tuple-element.61) | copy-start | bytes 2752516
  51.4 4.7 %copy-start.11 = (f32[256,896]{1,0:T(8,128)S(1)}, f32[256,896]{1,0:T(8,128)}, u32[]{:S(2)}) copy-start(f32[256,896]{1,0:T(8,128)} %get-tuple-element.63) | copy-start | bytes 2752516
  66.1 18.1 %copy-start.59 = (f32[256]{0:T(256)S(1)}, f32[256]{0:T(256)}, u32[]{:S(2)}) copy-start(f32[256]{0:T(256)} %get-tuple-element.16) | copy-start | bytes 3076
  66.1 18.2 %copy-start.60 = (f32[256]{0:T(256)S(1)}, f32[256]{0:T(256)}, u32[]{:S(2)}) copy-start(f32[256]{0:T(256)} %get-tuple-element.14) | copy-start | bytes 3076
  66.1 18.3 %copy-start.61 = (f32[256]{0:T(256)S(1)}, f32[256]{0:T(256)}, u32[]{:S(2)}) copy-start(f32[256]{0:T(256)} %get-tuple-element.12) | copy-start | bytes 3076
  66.2 18.3 %copy-start.62 = (f32[256]{0:T(256)S(1)}, f32[256]{0:T(256)}, u32[]{:S(2)}) copy-start(f32[256]{0:T(256)} %get-tuple-element.10) | copy-start | bytes 3076
  66.2 18.5 %copy-start.63 = (f32[256]{0:T(256)S(1)}, f32[256]{0:T(256)}, u32[]{:S(2)}) copy-start(f32[256]{0:T(256)} %get-tuple-element.6) | copy-start | bytes 3076
  66.2 18.6 %copy-start.64 = (f32[256]{0:T(256)S(1)}, f32[256]{0:T(256)}, u32[]{:S(2)}) copy-start(f32[256]{0:T(256)} %get-tuple-element.4) | copy-start | bytes 3076
  68.6 22.0 %copy-start.28 = (bf16[32,512]{0,1:T(8,128)(2,1)}, bf16[32,512]{0,1:T(8,128)(2,1)S(1)}, u32[]{:S(2)}) copy-start(bf16[32,512]{0,1:T(8,128)(2,1)S(1)} %collective-permute-done) | copy-start | bytes 98308
  68.6 4.4 %collective-permute-start.2 = (bf16[32,512]{0,1:T(8,128)(2,1)S(1)}, bf16[32,512]{0,1:T(8,128)(2,1)S(1)}, u32[]{:S(2)}, u32[]{:S(2)}) collective-permute-start(bf16[32,512]{0,1:T(8,128)(2,1)S(1)} %collective-permute-done), channel_id=1, source_target_pairs={{0,1},{1,2},{2,3},{3,4},{4,5},{5,6},{6,7},{7,0},{8,9},{9,10},{10,1... | collective-permute-start | bytes 98312 | tf_op jit(solution)/shard_map/ppermute | solution.py:15
  69.0 16.6 %copy-start.38 = (f32[896]{0:T(1024)}, f32[896]{0:T(1024)S(1)}, u32[]{:S(2)}) copy-start(f32[896]{0:T(1024)S(1)} %broadcast_maximum_fusion) | copy-start | bytes 10756
  69.0 4.5 %collective-permute-start.3 = (bf16[32,512]{0,1:T(8,128)(2,1)}, bf16[32,512]{0,1:T(8,128)(2,1)S(1)}, u32[]{:S(2)}, u32[]{:S(2)}) collective-permute-start(bf16[32,512]{0,1:T(8,128)(2,1)} %collective-permute-done.1), channel_id=1, source_target_pairs={{0,7},{1,0},{2,1},{3,2},{4,3},{5,4},{6,5},{7,6},{8,15},{9,8},{10,9... | collective-permute-start | bytes 98312 | tf_op jit(solution)/shard_map/ppermute | solution.py:18
  73.0 4.4 %copy-start.29 = (bf16[32,512]{0,1:T(8,128)(2,1)}, bf16[32,512]{0,1:T(8,128)(2,1)S(1)}, u32[]{:S(2)}) copy-start(bf16[32,512]{0,1:T(8,128)(2,1)S(1)} %collective-permute-done.2) | copy-start | bytes 98308
  73.0 4.4 %collective-permute-start.4 = (bf16[32,512]{0,1:T(8,128)(2,1)S(1)}, bf16[32,512]{0,1:T(8,128)(2,1)S(1)}, u32[]{:S(2)}, u32[]{:S(2)}) collective-permute-start(bf16[32,512]{0,1:T(8,128)(2,1)S(1)} %collective-permute-done.2), channel_id=1, source_target_pairs={{0,1},{1,2},{2,3},{3,4},{4,5},{5,6},{6,7},{7,0},{8,9},{9,10},{10,1... | collective-permute-start | bytes 98312 | tf_op jit(solution)/shard_map/ppermute | solution.py:15
  73.5 24.6 %collective-permute-start.5 = (bf16[32,512]{0,1:T(8,128)(2,1)S(1)}, bf16[32,512]{0,1:T(8,128)(2,1)}, u32[]{:S(2)}, u32[]{:S(2)}) collective-permute-start(bf16[32,512]{0,1:T(8,128)(2,1)S(1)} %collective-permute-done.3), channel_id=1, source_target_pairs={{0,7},{1,0},{2,1},{3,2},{4,3},{5,4},{6,5},{7,6},{8,15},{9,8},{10,9... | collective-permute-start | bytes 98312 | tf_op jit(solution)/shard_map/ppermute | solution.py:18
  77.4 22.4 %collective-permute-start.6 = (bf16[32,512]{0,1:T(8,128)(2,1)S(1)}, bf16[32,512]{0,1:T(8,128)(2,1)}, u32[]{:S(2)}, u32[]{:S(2)}) collective-permute-start(bf16[32,512]{0,1:T(8,128)(2,1)S(1)} %collective-permute-done.4), channel_id=1, source_target_pairs={{0,1},{1,2},{2,3},{3,4},{4,5},{5,6},{6,7},{7,0},{8,9},{9,10},{10,1... | collective-permute-start | bytes 98312 | tf_op jit(solution)/shard_map/ppermute | solution.py:15
  85.6 5.1 %copy-start.27 = (bf16[32,512]{0,1:T(8,128)(2,1)S(1)}, bf16[32,512]{0,1:T(8,128)(2,1)}, u32[]{:S(2)}) copy-start(bf16[32,512]{0,1:T(8,128)(2,1)} %copy-done.26) | copy-start | bytes 98308
  87.9 8.4 %copy-start.30 = (bf16[32,512]{0,1:T(8,128)(2,1)S(1)}, bf16[32,512]{0,1:T(8,128)(2,1)}, u32[]{:S(2)}) copy-start(bf16[32,512]{0,1:T(8,128)(2,1)} %copy-done.29) | copy-start | bytes 98308
  91.6 9.9 %copy-start.42 = (f32[896]{0:T(1024)S(1)}, f32[896]{0:T(1024)}, u32[]{:S(2)}) copy-start(f32[896]{0:T(1024)} %get-tuple-element.35) | copy-start | bytes 10756
  91.6 12.1 %copy-start.43 = (f32[896]{0:T(1024)S(1)}, f32[896]{0:T(1024)}, u32[]{:S(2)}) copy-start(f32[896]{0:T(1024)} %get-tuple-element.33) | copy-start | bytes 10756
  96.3 9.6 %copy-start.44 = (f32[896]{0:T(1024)S(1)}, f32[896]{0:T(1024)}, u32[]{:S(2)}) copy-start(f32[896]{0:T(1024)} %get-tuple-element.31) | copy-start | bytes 10756
  101.4 4.6 %copy-start.5 = (f32[896,256]{0,1:T(8,128)S(1)}, f32[896,256]{0,1:T(8,128)}, u32[]{:S(2)}) copy-start(f32[896,256]{0,1:T(8,128)} %copy-done.4) | copy-start | bytes 2752516
  101.4 5.5 %copy-start.3 = (f32[896,256]{0,1:T(8,128)S(1)}, f32[896,256]{0,1:T(8,128)}, u32[]{:S(2)}) copy-start(f32[896,256]{0,1:T(8,128)} %copy-done.2) | copy-start | bytes 2752516
  101.4 5.5 %copy-start.33 = (f32[896]{0:T(1024)S(1)}, f32[896]{0:T(1024)}, u32[]{:S(2)}) copy-start(f32[896]{0:T(1024)} %copy-done.32) | copy-start | bytes 10756
  101.4 5.5 %copy-start.45 = (f32[896]{0:T(1024)S(1)}, f32[896]{0:T(1024)}, u32[]{:S(2)}) copy-start(f32[896]{0:T(1024)} %get-tuple-element.29) | copy-start | bytes 10756
  103.7 4.2 %copy-start.1 = (f32[896,256]{0,1:T(8,128)S(1)}, f32[896,256]{0,1:T(8,128)}, u32[]{:S(2)}) copy-start(f32[896,256]{0,1:T(8,128)} %copy-done) | copy-start | bytes 2752516
  103.7 4.2 %copy-start.35 = (f32[896]{0:T(1024)S(1)}, f32[896]{0:T(1024)}, u32[]{:S(2)}) copy-start(f32[896]{0:T(1024)} %copy-done.34) | copy-start | bytes 10756
  103.7 4.2 %copy-start.46 = (f32[896]{0:T(1024)S(1)}, f32[896]{0:T(1024)}, u32[]{:S(2)}) copy-start(f32[896]{0:T(1024)} %get-tuple-element.27) | copy-start | bytes 10756
  106.9 9.4 %copy-start.48 = (f32[896]{0:T(1024)S(1)}, f32[896]{0:T(1024)}, u32[]{:S(2)}) copy-start(f32[896]{0:T(1024)} %get-tuple-element.23) | copy-start | bytes 10756
  108.9 15.6 %copy-start.39 = (f32[896]{0:T(1024)S(1)}, f32[896]{0:T(1024)}, u32[]{:S(2)}) copy-start(f32[896]{0:T(1024)} %copy-done.38) | copy-start | bytes 10756
  108.9 15.6 %copy-start.49 = (f32[896]{0:T(1024)S(1)}, f32[896]{0:T(1024)}, u32[]{:S(2)}) copy-start(f32[896]{0:T(1024)} %get-tuple-element.21) | copy-start | bytes 10756
  109.9 15.6 %copy-start.31 = (f32[8,896]{1,0:T(8,128)S(1)}, f32[8,896]{1,0:T(8,128)}, u32[]{:S(2)}) copy-start(f32[8,896]{1,0:T(8,128)} %stack.112) | copy-start | bytes 86020
  109.9 9.7 %all-to-all-start.3 = ((f32[8,1,256]{2,1,0:T(1,128)}), f32[8,1,256]{2,1,0:T(1,128)S(1)}, u32[]{:S(2)}, u32[]{:S(2)}) async-start(f32[8,1,256]{2,1,0:T(1,128)} %reshape.487), calls=%async_computation.3 | async-start | bytes 16384 | tf_op jit(solution)/shard_map/all_to_all | solution.py:114
  119.6 13.1 %all-to-all-start.1 = ((f32[8,1,16384]{2,1,0:T(1,128)}), f32[8,1,16384]{2,1,0:T(1,128)S(1)}, u32[]{:S(2)}, u32[]{:S(2)}) async-start(f32[8,1,16384]{2,1,0:T(1,128)} %reshape.483), calls=%async_computation.1 | async-start | bytes 1048576 | tf_op jit(solution)/shard_map/all_to_all | solution.py:115
  132.7 28.0 %all-to-all-start = ((bf16[4,224,512]{2,1,0:T(8,128)(2,1)}), bf16[4,224,512]{2,1,0:T(8,128)(2,1)S(1)}, u32[]{:S(2)}, u32[]{:S(2)}) async-start(bf16[4,224,512]{2,1,0:T(8,128)(2,1)} %copy.46), calls=%async_computation | async-start | bytes 1835008 | tf_op jit(solution)/shard_map/all_to_all | solution.py:75
  (28 other events, 81.5 us)
